TPU v7x, 32 devices: a whole 2x2x4 slice. The times are simulated.
32 devices in a mesh: dp: 4 (over x, core), seq: 2 (over y), tensor: 4 (over z).
Axes of the slice: x: 2, y: 2, z: 4, core: 2. Of those that a mesh axis runs over, the one named last changes fastest.
Arguments:
- tokens: bfloat16 [8, 1024, 768], P('dp', 'seq'), may hold values from -6 to 6
- segments: int32 [8, 1024], P('dp'), may hold values from 0 to 2, never falling along the last dimension, each value on 1 to 512 neighbouring positions
- projections: bfloat16 [3, 768, 768], P(None, ('dp', 'seq'), 'tensor'), may hold values from -0.21875 to 0.21875
- offsets: bfloat16 [2, 12, 64], P(None, 'tensor', ('dp', 'seq')), may hold values from -3 to 3
- mixing: bfloat16 [768, 768], P('tensor', ('dp', 'seq')), may hold values from -2.5 to 2.5
- upward: bfloat16 [768, 3072], P(('dp', 'seq'), 'tensor'), may hold values from -0.21875 to 0.21875
- thresholds: bfloat16 [48, 64], P('tensor', ('dp', 'seq')), may hold values from -3 to 3
- downward: bfloat16 [3072, 768], P('tensor', ('dp', 'seq')), may hold values from -0.109375 to 0.109375
- scales: bfloat16 [2, 768], P(None, ('dp', 'seq')), may hold values from 0.099609375 to 1.8984375
- shifts: bfloat16 [2, 768], P(None, ('dp', 'seq')), may hold values from -2 to 2
- biases: bfloat16 [2, 768], P(None, ('dp', 'seq')), may hold values from -2 to 2
- cotangent: bfloat16 [8, 1024, 768], P('dp', 'seq'), may hold values from -6 to 6
Outputs:
- result: bfloat16 [8, 1024, 768], P('dp', 'seq')
- tokens_grad: bfloat16 [8, 1024, 768], P('dp', 'seq')
- projections_grad: float32 [3, 768, 768], P(None, ('dp', 'seq'), 'tensor')
- offsets_grad: float32 [2, 12, 64], P(None, 'tensor', ('dp', 'seq'))
- mixing_grad: float32 [768, 768], P('tensor', ('dp', 'seq'))
- upward_grad: float32 [768, 3072], P(('dp', 'seq'), 'tensor')
- thresholds_grad: float32 [48, 64], P('tensor', ('dp', 'seq'))
- downward_grad: float32 [3072, 768], P('tensor', ('dp', 'seq'))
- scales_grad: float32 [2, 768], P(None, ('dp', 'seq'))
- shifts_grad: float32 [2, 768], P(None, ('dp', 'seq'))
- biases_grad: float32 [2, 768], P(None, ('dp', 'seq'))
Inputs may be any that keep to these rules, and one draw needn't show every extreme that they name: `segments`: ids never fall along a sequence; each document holds 1 to 512 tokens, and one holds exactly 512.
All inputs are finite; a program needn't handle non-finite values.
Results may differ from a plain program's by a relative error of at most 0.012.
Values may be sent and summed in bfloat16 or wider, within the bound.
A program may use at most 128 MiB of HBM per device.

v0:
```python
import jax
import jax.numpy as jnp
from jax import lax
from jax.sharding import PartitionSpec as P


def norm_rows(values, gain_row, shift_row):
    average = jnp.mean(values, axis=-1, keepdims=True)
    centered = values - average
    variance = jnp.mean(centered * centered, axis=-1, keepdims=True)
    return centered * lax.rsqrt(variance + 1e-05) * gain_row + shift_row


def gelu_tanh(values):
    return (
        0.5
        * values
        * (1.0 + jnp.tanh(0.7978845608028654 * (values + 0.044715 * values * values * values)))
    )


def head_scores(query_head, key_head, allowed):
    scores = (
        jnp.einsum("qe,ke->qk", query_head, key_head, preferred_element_type=jnp.float32) * 0.125
    )
    return jnp.where(allowed, scores, -1e30)


def accumulate(running, addition):
    return addition if running is None else running + addition


def per_device(
    tokens,
    segments,
    projections,
    offsets,
    mixing,
    upward,
    thresholds,
    downward,
    scales,
    shifts,
    biases,
    cotangent,
):
    micro = tokens.shape[0]
    block_len = tokens.shape[1]
    seq_len = segments.shape[1]
    head_size = offsets.shape[2] * lax.axis_size(("dp", "seq"))
    start = lax.axis_index("seq") * block_len
    query_pos = start + jnp.arange(block_len, dtype=jnp.int32)
    key_pos = jnp.arange(seq_len, dtype=jnp.int32)
    saved = []
    results = []
    for batch_index in range(micro):
        gathered = (
            lax.all_gather(projections, ("dp", "seq"), axis=1, tiled=True),
            lax.all_gather(offsets, ("dp", "seq"), axis=2, tiled=True),
            lax.all_gather(mixing, ("dp", "seq"), axis=1, tiled=True),
            lax.all_gather(upward, ("dp", "seq"), axis=0, tiled=True),
            lax.all_gather(thresholds, ("dp", "seq"), axis=1, tiled=True),
            lax.all_gather(downward, ("dp", "seq"), axis=1, tiled=True),
            lax.all_gather(scales, ("dp", "seq"), axis=1, tiled=True),
            lax.all_gather(shifts, ("dp", "seq"), axis=1, tiled=True),
            lax.all_gather(biases, ("dp", "seq"), axis=1, tiled=True),
        )
        (
            entry_weights,
            entry_offsets,
            mixer_weights,
            upward_full,
            threshold_full,
            downward_full,
            scale_full,
            shift_full,
            biases_full,
        ) = gathered
        scale_rows = scale_full.astype(jnp.float32)
        shift_rows = shift_full.astype(jnp.float32)
        bias_rows = biases_full.astype(jnp.float32)
        offset_rows = entry_offsets.astype(jnp.float32).reshape(2, -1)
        inputs = tokens[batch_index].astype(jnp.float32)
        normed = norm_rows(inputs, scale_rows[0], shift_rows[0]).astype(jnp.bfloat16)
        stacked = jnp.einsum(
            "cd,tde->tce", normed, entry_weights, preferred_element_type=jnp.float32
        )
        query_b = (stacked[0] + offset_rows[0]).astype(jnp.bfloat16)
        key_b = stacked[1].astype(jnp.bfloat16)
        value_b = (stacked[2] + offset_rows[1]).astype(jnp.bfloat16)
        key_full, value_full = (
            lax.all_gather(key_b, "seq", axis=0, tiled=True),
            lax.all_gather(value_b, "seq", axis=0, tiled=True),
        )
        seg_row = segments[batch_index]
        own_seg = lax.dynamic_slice_in_dim(seg_row, start, block_len)
        allowed = (key_pos[None, :] <= query_pos[:, None]) & (seg_row[None, :] == own_seg[:, None])
        head_count = query_b.shape[1] // head_size
        pieces = []
        totals = []
        for head_index in range(head_count):
            columns = slice(head_index * head_size, (head_index + 1) * head_size)
            scores = head_scores(query_b[:, columns], key_full[:, columns], allowed)
            log_total = jax.nn.logsumexp(scores, axis=1, keepdims=True)
            weights_b = jnp.exp(scores - log_total).astype(jnp.bfloat16)
            pieces.append(
                jnp.dot(weights_b, value_full[:, columns], preferred_element_type=jnp.float32)
            )
            totals.append(log_total)
        attended = jnp.concatenate(pieces, axis=1).astype(jnp.bfloat16)
        branch = lax.psum(
            jnp.dot(attended, mixer_weights, preferred_element_type=jnp.float32), "tensor"
        )
        hidden = inputs + branch + bias_rows[0]
        normed2 = norm_rows(hidden, scale_rows[1], shift_rows[1]).astype(jnp.bfloat16)
        pre_act = jnp.dot(
            normed2, upward_full, preferred_element_type=jnp.float32
        ) + threshold_full.astype(jnp.float32).reshape(-1)
        activated = gelu_tanh(pre_act).astype(jnp.bfloat16)
        lifted = lax.psum(
            jnp.dot(activated, downward_full, preferred_element_type=jnp.float32).astype(
                jnp.bfloat16
            ),
            "tensor",
        ).astype(jnp.float32)
        results.append((hidden + lifted + bias_rows[1]).astype(jnp.bfloat16))
        kept_keys = (key_b, value_b)
        saved.append(
            (
                inputs,
                normed,
                query_b,
                kept_keys,
                allowed,
                totals,
                attended,
                hidden,
                normed2,
                pre_act,
                activated,
            )
        )
    entry_acc = None
    offset_acc = None
    mixer_acc = None
    upward_acc = None
    threshold_acc = None
    downward_acc = None
    scale_acc = None
    shift_acc = None
    bias_acc = None
    input_grads = []
    for batch_index in range(micro):
        gathered = (
            lax.all_gather(projections, ("dp", "seq"), axis=1, tiled=True),
            lax.all_gather(offsets, ("dp", "seq"), axis=2, tiled=True),
            lax.all_gather(mixing, ("dp", "seq"), axis=1, tiled=True),
            lax.all_gather(upward, ("dp", "seq"), axis=0, tiled=True),
            lax.all_gather(thresholds, ("dp", "seq"), axis=1, tiled=True),
            lax.all_gather(downward, ("dp", "seq"), axis=1, tiled=True),
            lax.all_gather(scales, ("dp", "seq"), axis=1, tiled=True),
            lax.all_gather(shifts, ("dp", "seq"), axis=1, tiled=True),
            lax.all_gather(biases, ("dp", "seq"), axis=1, tiled=True),
        )
        (
            entry_weights,
            entry_offsets,
            mixer_weights,
            upward_full,
            threshold_full,
            downward_full,
            scale_full,
            shift_full,
            biases_full,
        ) = gathered
        scale_rows = scale_full.astype(jnp.float32)
        shift_rows = shift_full.astype(jnp.float32)
        (
            inputs,
            normed,
            query_b,
            kept_keys,
            allowed,
            totals,
            attended,
            hidden,
            normed2,
            pre_act,
            activated,
        ) = saved[batch_index]
        grad_out = cotangent[batch_index].astype(jnp.float32)
        grad_out_b = grad_out.astype(jnp.bfloat16)
        downward_acc = accumulate(
            downward_acc,
            jnp.einsum("cf,cd->fd", activated, grad_out_b, preferred_element_type=jnp.float32),
        )
        grad_act = jnp.einsum(
            "cd,fd->cf", grad_out_b, downward_full, preferred_element_type=jnp.float32
        )
        unused, gelu_back = jax.vjp(gelu_tanh, pre_act)
        grad_pre = gelu_back(grad_act)[0].astype(jnp.bfloat16)
        threshold_acc = accumulate(threshold_acc, jnp.sum(grad_pre.astype(jnp.float32), axis=0))
        upward_acc = accumulate(
            upward_acc,
            jnp.einsum("cd,cf->df", normed2, grad_pre, preferred_element_type=jnp.float32),
        )
        grad_normed2 = lax.psum(
            jnp.einsum("cf,df->cd", grad_pre, upward_full, preferred_element_type=jnp.float32),
            "tensor",
        )
        unused, second_back = jax.vjp(norm_rows, hidden, scale_rows[1], shift_rows[1])
        grad_from_norm, scale_second, shift_second = second_back(grad_normed2)
        grad_hidden = grad_out + grad_from_norm
        grad_hidden_b = grad_hidden.astype(jnp.bfloat16)
        mixer_acc = accumulate(
            mixer_acc,
            jnp.einsum("ce,cd->ed", attended, grad_hidden_b, preferred_element_type=jnp.float32),
        )
        grad_attended = jnp.einsum(
            "cd,ed->ce", grad_hidden_b, mixer_weights, preferred_element_type=jnp.float32
        ).astype(jnp.bfloat16)
        own_keys, own_values = kept_keys
        key_full, value_full = (
            lax.all_gather(own_keys, "seq", axis=0, tiled=True),
            lax.all_gather(own_values, "seq", axis=0, tiled=True),
        )
        head_count = query_b.shape[1] // head_size
        query_grads = []
        key_grads = []
        value_grads = []
        for head_index in range(head_count):
            columns = slice(head_index * head_size, (head_index + 1) * head_size)
            scores = head_scores(query_b[:, columns], key_full[:, columns], allowed)
            probs = jnp.exp(scores - totals[head_index])
            grad_slice = grad_attended[:, columns]
            grad_probs = jnp.einsum(
                "qe,ke->qk", grad_slice, value_full[:, columns], preferred_element_type=jnp.float32
            )
            delta_rows = jnp.sum(probs * grad_probs, axis=1, keepdims=True)
            grad_scores = (probs * (grad_probs - delta_rows)).astype(jnp.bfloat16)
            query_grads.append(
                jnp.einsum(
                    "qk,ke->qe",
                    grad_scores,
                    key_full[:, columns],
                    preferred_element_type=jnp.float32,
                )
                * 0.125
            )
            probs_b = probs.astype(jnp.bfloat16)
            value_grads.append(
                jnp.einsum("qk,qe->ke", probs_b, grad_slice, preferred_element_type=jnp.float32)
            )
            key_grads.append(
                jnp.einsum(
                    "qk,qe->ke",
                    grad_scores,
                    query_b[:, columns],
                    preferred_element_type=jnp.float32,
                )
                * 0.125
            )
        key_grad_full = jnp.concatenate(key_grads, axis=1)
        value_grad_full = jnp.concatenate(value_grads, axis=1)
        key_grad, value_grad = (
            lax.psum_scatter(key_grad_full, "seq", scatter_dimension=0, tiled=True),
            lax.psum_scatter(value_grad_full, "seq", scatter_dimension=0, tiled=True),
        )
        triple = jnp.stack([jnp.concatenate(query_grads, axis=1), key_grad, value_grad]).astype(
            jnp.bfloat16
        )
        triple_sums = jnp.sum(triple.astype(jnp.float32), axis=1)
        offset_acc = accumulate(offset_acc, jnp.stack([triple_sums[0], triple_sums[2]]))
        entry_acc = accumulate(
            entry_acc, jnp.einsum("cd,tce->tde", normed, triple, preferred_element_type=jnp.float32)
        )
        grad_normed = lax.psum(
            jnp.einsum("tce,tde->cd", triple, entry_weights, preferred_element_type=jnp.float32),
            "tensor",
        )
        unused, first_back = jax.vjp(norm_rows, inputs, scale_rows[0], shift_rows[0])
        grad_inputs, scale_first, shift_first = first_back(grad_normed)
        input_grads.append((grad_hidden + grad_inputs).astype(jnp.bfloat16))
        scale_acc = accumulate(scale_acc, jnp.stack([scale_first, scale_second]))
        shift_acc = accumulate(shift_acc, jnp.stack([shift_first, shift_second]))
        bias_acc = accumulate(
            bias_acc, jnp.stack([jnp.sum(grad_hidden, axis=0), jnp.sum(grad_out, axis=0)])
        )
    offset_acc = offset_acc.reshape(entry_offsets.shape)
    threshold_acc = threshold_acc.reshape(threshold_full.shape)
    summed = (
        lax.psum_scatter(entry_acc, ("dp", "seq"), scatter_dimension=1, tiled=True),
        lax.psum_scatter(offset_acc, ("dp", "seq"), scatter_dimension=2, tiled=True),
        lax.psum_scatter(mixer_acc, ("dp", "seq"), scatter_dimension=1, tiled=True),
        lax.psum_scatter(upward_acc, ("dp", "seq"), scatter_dimension=0, tiled=True),
        lax.psum_scatter(threshold_acc, ("dp", "seq"), scatter_dimension=1, tiled=True),
        lax.psum_scatter(downward_acc, ("dp", "seq"), scatter_dimension=1, tiled=True),
        lax.psum_scatter(scale_acc, ("dp", "seq"), scatter_dimension=1, tiled=True),
        lax.psum_scatter(shift_acc, ("dp", "seq"), scatter_dimension=1, tiled=True),
        lax.psum_scatter(bias_acc, ("dp", "seq"), scatter_dimension=1, tiled=True),
    )
    return (
        jnp.stack(results),
        jnp.stack(input_grads),
        summed[0],
        summed[1],
        summed[2],
        summed[3],
        summed[4],
        summed[5],
        summed[6],
        summed[7],
        summed[8],
    )


def solution(mesh):
    placed = (
        P("dp", "seq", None),
        P("dp", None),
        P(None, ("dp", "seq"), "tensor"),
        P(None, "tensor", ("dp", "seq")),
        P("tensor", ("dp", "seq")),
        P(("dp", "seq"), "tensor"),
        P("tensor", ("dp", "seq")),
        P("tensor", ("dp", "seq")),
        P(None, ("dp", "seq")),
        P(None, ("dp", "seq")),
        P(None, ("dp", "seq")),
        P("dp", "seq", None),
    )
    return jax.shard_map(
        per_device,
        mesh=mesh,
        in_specs=placed,
        out_specs=(
            P("dp", "seq", None),
            P("dp", "seq", None),
            P(None, ("dp", "seq"), "tensor"),
            P(None, "tensor", ("dp", "seq")),
            P("tensor", ("dp", "seq")),
            P(("dp", "seq"), "tensor"),
            P("tensor", ("dp", "seq")),
            P("tensor", ("dp", "seq")),
            P(None, ("dp", "seq")),
            P(None, ("dp", "seq")),
            P(None, ("dp", "seq")),
        ),
        check_vma=False,
    )
```

profile of v0, /device:TPU:0, one launch (start us, length us, event | category | flops | bytes accessed | tf_op | source)
XLA Modules:
  0.0 897.6 jit_solution(6401317190653829994)
XLA Ops:
  9.0 13.2 %all-gather.2 = bf16[8,96,2]{1,2,0:T(2,128)(2,1)S(1)} all-gather(bf16[1,96,2]{1,2,0:T(2,128)(2,1)} %bitcast.306), channel_id=1, replica_groups=mesh['dp'=4,'seq'=2,'tensor'=4] {'dp','seq'}, dimensions={0}, use_global_device_ids=true | all-gather | bytes 3456 | tf_op jit(solution)/shard_map/all_gather | solution.py:64
  22.3 10.9 %all-gather.3 = bf16[8,96,2]{1,2,0:T(2,128)(2,1)S(1)} all-gather(bf16[1,96,2]{1,2,0:T(2,128)(2,1)} %bitcast.307), channel_id=1, replica_groups=mesh['dp'=4,'seq'=2,'tensor'=4] {'dp','seq'}, dimensions={0}, use_global_device_ids=true | all-gather | bytes 3456 | tf_op jit(solution)/shard_map/all_gather | solution.py:65
  36.2 12.5 %all_gather.29 = bf16[2,3,64]{1,0,2:T(2,128)(2,1)S(1)} all-gather(bf16[2,3,8]{1,0,2:T(2,128)(2,1)S(1)} %copy.73), channel_id=1, replica_groups=mesh['dp'=4,'seq'=2,'tensor'=4] {'dp','seq'}, dimensions={2}, use_global_device_ids=true | all-gather | bytes 864 | tf_op jit(solution)/shard_map/all_gather | solution.py:59
  49.3 23.8 %all_gather.28 = bf16[3,768,192]{2,0,1:T(4,128)(2,1)S(1)} all-gather(bf16[3,96,192]{2,0,1:T(4,128)(2,1)S(1)} %copy.71), channel_id=1, replica_groups=mesh['dp'=4,'seq'=2,'tensor'=4] {'dp','seq'}, dimensions={1}, use_global_device_ids=true | all-gather | bytes 995328 | tf_op jit(solution)/shard_map/all_gather | solution.py:58
  75.7 2.1 fusion.175
  79.8 8.4 all-gather
  88.2 2.1 fusion.79
  92.3 2.1 fusion.194
  94.4 2.0 fusion.195
  96.4 7.5 all-gather.1
  110.1 15.6 %all_gather.32 = bf16[192,768]{0,1:T(8,128)(2,1)S(1)} all-gather(bf16[192,96]{0,1:T(8,128)(2,1)S(1)} %copy.76), channel_id=1, replica_groups=mesh['dp'=4,'seq'=2,'tensor'=4] {'dp','seq'}, dimensions={1}, use_global_device_ids=true | all-gather | bytes 331776 | tf_op jit(solution)/shard_map/all_gather | solution.py:60
  125.8 8.2 all_gather.74
  134.0 8.1 all_gather.31
  142.2 2.2 exponential_reduce_fusion.3
  159.2 11.3 %all-gather.4 = bf16[8,96,2]{1,2,0:T(2,128)(2,1)S(1)} all-gather(bf16[1,96,2]{1,2,0:T(2,128)(2,1)S(1)} %bitcast.308), channel_id=1, replica_groups=mesh['dp'=4,'seq'=2,'tensor'=4] {'dp','seq'}, dimensions={0}, use_global_device_ids=true | all-gather | bytes 3456 | tf_op jit(solution)/shard_map/all_gather | solution.py:66
  171.3 16.3 %all_gather.35 = bf16[12,64]{0,1:T(8,128)(2,1)S(1)} all-gather(bf16[12,8]{0,1:T(8,128)(2,1)S(1)} %copy-done.131), channel_id=1, replica_groups=mesh['dp'=4,'seq'=2,'tensor'=4] {'dp','seq'}, dimensions={1}, use_global_device_ids=true | all-gather | bytes 1728 | tf_op jit(solution)/shard_map/all_gather | solution.py:62
  188.3 91.5 %all-reduce.16.cloned.1.call-done = (f32[512,768]{1,0:T(8,128)}, f32[512,768]{1,0:T(8,128)}) async-done(((f32[512,768]{1,0:T(8,128)}, f32[512,768]{1,0:T(8,128)}), (f32[512,768]{1,0:T(8,128)}, f32[512,768]{1,0:T(8,128)})) %all-reduce.16.cloned.1.call-update) | async-done | bytes 3145744 | tf_op jit(solution)/shard_map/psum | solution.py:111
  279.8 2.4 fusion.184
  284.5 3.9 convolution_add_fusion.3
  288.5 2.1 convolution_add_fusion.2
  290.6 4.5 convert_reduce_fusion.5
  295.1 2.4 convert_reduce_fusion.4
  301.6 3.9 convolution_convert_fusion.1
  307.7 114.4 %all-reduce.14.cloned.1.call-done = (f32[512,768]{1,0:T(8,128)}, f32[512,768]{1,0:T(8,128)}) async-done(((f32[512,768]{1,0:T(8,128)}, f32[512,768]{1,0:T(8,128)}), (f32[512,768]{1,0:T(8,128)}, f32[512,768]{1,0:T(8,128)})) %all-reduce.14.cloned.1.call-update) | async-done | bytes 3145744 | tf_op jit(solution)/shard_map/psum | solution.py:207
  422.1 3.6 multiply_reduce_fusion.6
  426.9 66.1 %all-reduce.18.cloned.1.call-done = (bf16[512,768]{1,0:T(8,128)(2,1)}, bf16[512,768]{1,0:T(8,128)(2,1)}) async-done(((bf16[512,768]{1,0:T(8,128)(2,1)}, bf16[512,768]{1,0:T(8,128)(2,1)}), (bf16[512,768]{1,0:T(8,128)(2,1)}, bf16[512,768]{1,0:T(8,128)(2,1)})) %all-reduce.18.cloned.1.call-update) | async-done | bytes 1572880 | tf_op jit(solution)/shard_map/psum | solution.py:120
  493.1 5.0 fusion.183
  510.3 2.4 multiply_reduce_fusion.3
  512.7 2.4 multiply_reduce_fusion.4
  516.1 2.8 multiply_convert_fusion.3
  522.7 2.8 multiply_convert_fusion.4
  530.6 2.1 pad_maximum_fusion.2
  532.6 2.3 multiply_reduce_fusion
  535.5 2.4 convolution_multiply_fusion
  537.9 2.4 multiply_reduce_fusion.1
  540.4 2.4 multiply_reduce_fusion.2
  543.3 2.8 multiply_convert_fusion.1
  550.0 2.5 fusion.50
  552.4 2.3 fusion.49
  555.8 2.1 fusion.53
  565.5 6.5 reduce-scatter.24.cloned.1.call-done
  573.7 3.3 convolution_bitcast_fusion.1
  577.0 14.7 %reduce-scatter.28.cloned.1.call-done = f32[512,192]{0,1:T(8,128)} async-done(((f32[1024,192]{0,1:T(8,128)}), f32[512,192]{0,1:T(8,128)}) %reduce-scatter.28.cloned.1.call-update) | async-done | bytes 393232 | tf_op jit(solution)/shard_map/reduce_scatter | solution.py:266
  593.3 3.3 convolution_bitcast_fusion
  597.3 2.5 fusion.181
  602.1 3.2 fusion.86
  605.3 2.7 convolution_add_fusion.4
  608.0 2.2 copy.89
  612.4 2.1 add_bitcast_fusion
  614.5 4.3 copy.85
  618.8 4.7 reshape.318
  623.7 4.1 fusion.66
  630.1 88.1 %all-reduce.12.cloned.1.call-done = (f32[512,768]{1,0:T(8,128)}, f32[512,768]{1,0:T(8,128)}) async-done(((f32[512,768]{1,0:T(8,128)}, f32[512,768]{1,0:T(8,128)}), (f32[512,768]{1,0:T(8,128)}, f32[512,768]{1,0:T(8,128)})) %all-reduce.12.cloned.1.call-update) | async-done | bytes 3145744 | tf_op jit(solution)/shard_map/psum | solution.py:277
  718.3 2.9 fusion.31
  722.6 2.3 fusion.29
  730.3 4.9 convolution_add_fusion
  735.2 2.8 fusion.179
  738.1 2.5 convolution_add_fusion.1
  743.8 2.7 pad_maximum_fusion
  752.4 24.1 %all-reduce.2 = (f32[2,3,64]{2,1,0:T(4,128)S(1)}, f32[12,64]{1,0:T(8,128)S(1)}) all-reduce(f32[2,3,64]{2,1,0:T(4,128)S(1)} %maximum_add_fusion.3, f32[12,64]{1,0:T(8,128)} %add.400), channel_id=9, replica_groups=mesh['dp'=4,'seq'=2,'tensor'=4] {'dp','seq'}, use_global_device_ids=true, to_apply=%region_49.50.clone | all-reduce | flops 1152 | bytes 9216
  781.2 3.7 fusion.56
  787.6 9.6 %reduce-scatter.42.cloned.1.call-done = f32[96,2]{1,0:T(8,128)} async-done(((f32[768,2]{1,0:T(8,128)}), f32[96,2]{1,0:T(8,128)}) %reduce-scatter.42.cloned.1.call-update) | async-done | bytes 784
  798.7 45.3 %reduce-scatter.34.cloned.1.call-done = f32[768,96]{0,1:T(8,128)} async-done(((f32[768,768]{0,1:T(8,128)}), f32[768,96]{0,1:T(8,128)}) %reduce-scatter.34.cloned.1.call-update) | async-done | bytes 294928 | tf_op jit(solution)/shard_map/reduce_scatter | solution.py:297
  843.9 46.1 %reduce-scatter.32.cloned.1.call-done = f32[96,768]{1,0:T(8,128)} async-done(((f32[768,768]{1,0:T(8,128)}), f32[96,768]{1,0:T(8,128)}) %reduce-scatter.32.cloned.1.call-update) | async-done | bytes 294928 | tf_op jit(solution)/shard_map/reduce_scatter | solution.py:295
  (468 shorter events, 113.3 us)
Async XLA Ops:
  8.0 27.0 %copy-start = (bf16[2,512,768]{2,1,0:T(8,128)(2,1)S(1)}, bf16[2,512,768]{2,1,0:T(8,128)(2,1)}, u32[]{:S(2)}) copy-start(bf16[2,512,768]{2,1,0:T(8,128)(2,1)} %param.12) | copy-start | bytes 4718596
  8.0 271.8 %all-reduce.16.cloned.1.call-start = ((), (), s32[]{:S(2)}) async-start(), calls=%async_computation.26 | async-start | bytes 6291456 | tf_op jit(solution)/shard_map/psum | solution.py:111
  33.3 15.8 %copy-start.75 = (bf16[3,96,192]{2,1,0:T(8,128)(2,1)S(1)}, bf16[3,96,192]{2,1,0:T(8,128)(2,1)}, u32[]{:S(2)}) copy-start(bf16[3,96,192]{2,1,0:T(8,128)(2,1)} %param.14) | copy-start | bytes 331780
  35.0 40.7 %copy-start.90 = (f32[512]{0:T(512)}, f32[512]{0:T(512)S(1)}, u32[]{:S(2)}) copy-start(f32[512]{0:T(512)S(1)} %get-tuple-element.168) | copy-start | bytes 6148
  35.0 42.9 %copy-start.92 = (f32[512]{0:T(512)}, f32[512]{0:T(512)S(1)}, u32[]{:S(2)}) copy-start(f32[512]{0:T(512)S(1)} %get-tuple-element.169) | copy-start | bytes 6148
  35.6 39.5 %copy-start.110 = (f32[512]{0:T(512)}, f32[512]{0:T(512)S(1)}, u32[]{:S(2)}) copy-start(f32[512]{0:T(512)S(1)} %get-tuple-element.87) | copy-start | bytes 6148
  36.2 41.6 %copy-start.105 = (f32[512]{0:T(512)}, f32[512]{0:T(512)S(1)}, u32[]{:S(2)}) copy-start(f32[512]{0:T(512)S(1)} %fusion.151) | copy-start | bytes 6148
  36.2 39.5 %copy-start.107 = (f32[512]{0:T(512)}, f32[512]{0:T(512)S(1)}, u32[]{:S(2)}) copy-start(f32[512]{0:T(512)S(1)} %fusion.153) | copy-start | bytes 6148
  88.2 6.2 copy-start.45
  90.3 17.6 %copy-start.64 = (bf16[512,192]{0,1:T(8,128)(2,1)}, bf16[512,192]{0,1:T(8,128)(2,1)S(1)}, u32[]{:S(2)}) copy-start(bf16[512,192]{0,1:T(8,128)(2,1)S(1)} %get-tuple-element.126) | copy-start | bytes 589828
  107.9 17.8 %copy-start.63 = (bf16[512,192]{0,1:T(8,128)(2,1)S(1)}, bf16[512,192]{0,1:T(8,128)(2,1)}, u32[]{:S(2)}) copy-start(bf16[512,192]{0,1:T(8,128)(2,1)} %get-tuple-element.127) | copy-start | bytes 589828
  108.0 26.0 %copy-start.62 = (bf16[512,192]{0,1:T(8,128)(2,1)S(1)}, bf16[512,192]{0,1:T(8,128)(2,1)}, u32[]{:S(2)}) copy-start(bf16[512,192]{0,1:T(8,128)(2,1)} %get-tuple-element.138) | copy-start | bytes 589828
  125.7 18.6 %copy-start.14 = (f32[512,1024]{1,0:T(8,128)S(1)}, f32[512,1024]{1,0:T(8,128)}, u32[]{:S(2)}) copy-start(f32[512,1024]{1,0:T(8,128)} %get-tuple-element.149) | copy-start | bytes 6291460
  134.0 20.2 %copy-start.38 = (bf16[1024,192]{0,1:T(8,128)(2,1)}, bf16[1024,192]{0,1:T(8,128)(2,1)S(1)}, u32[]{:S(2)}) copy-start(bf16[1024,192]{0,1:T(8,128)(2,1)S(1)} %all_gather.74) | copy-start | bytes 1179652
  142.1 6.5 copy-start.40
  146.5 8.3 copy-start.71
  147.0 7.8 copy-start.72
  149.2 5.6 copy-start.73
  152.1 4.3 copy-start.68
  158.0 13.3 %copy-start.131 = (bf16[12,8]{0,1:T(8,128)(2,1)S(1)}, bf16[12,8]{0,1:T(8,128)(2,1)}, u32[]{:S(2)}) copy-start(bf16[12,8]{0,1:T(8,128)(2,1)} %param.18) | copy-start | bytes 580
  158.0 126.5 %all-gather.8.cloned.1.call-start = ((), (), s32[]{:S(2)}) async-start(), calls=%async_computation.11 | async-start | bytes 1327104 | tf_op jit(solution)/shard_map/all_gather | solution.py:61
  158.6 132.0 %all-gather.10.cloned.1.call-start = ((), (), s32[]{:S(2)}) async-start(), calls=%async_computation.12 | async-start | bytes 1327104 | tf_op jit(solution)/shard_map/all_gather | solution.py:63
  159.2 263.0 %all-reduce.14.cloned.1.call-start = ((), (), s32[]{:S(2)}) async-start(), calls=%async_computation.25 | async-start | bytes 6291456 | tf_op jit(solution)/shard_map/psum | solution.py:207
  282.2 140.0 %copy-start.19 = (f32[512,768]{1,0:T(8,128)}, f32[512,768]{1,0:T(8,128)S(1)}, u32[]{:S(2)}) copy-start(f32[512,768]{1,0:T(8,128)S(1)} %get-tuple-element.121) | copy-start | bytes 4718596
  282.2 210.9 %copy-start.97 = (f32[512]{0:T(512)}, f32[512]{0:T(512)S(1)}, u32[]{:S(2)}) copy-start(f32[512]{0:T(512)S(1)} %broadcast_multiply_fusion) | copy-start | bytes 6148
  290.6 4.5 copy-start.21
  290.6 4.5 copy-start.36
  290.6 4.5 copy-start.133
  295.1 4.4 copy-start.138
  301.5 191.6 %all-reduce.18.cloned.1.call-start = ((), (), s32[]{:S(2)}) async-start(), calls=%async_computation.27 | async-start | bytes 3145728 | tf_op jit(solution)/shard_map/psum | solution.py:120
  307.5 254.6 %reduce-scatter.26.cloned.1.call-start = ((), (), s32[]{:S(2)}) async-start(), calls=%async_computation.14 | async-start | bytes 1179648 | tf_op jit(solution)/shard_map/reduce_scatter | solution.py:267
  422.1 4.2 copy-start.115
  493.1 5.6 copy-start.22
  500.2 12.5 %copy-start.44 = (bf16[512,192]{0,1:T(8,128)(2,1)}, bf16[512,192]{0,1:T(8,128)(2,1)S(1)}, u32[]{:S(2)}) copy-start(bf16[512,192]{0,1:T(8,128)(2,1)S(1)} %convolution_convert_fusion.3) | copy-start | bytes 589828
  516.0 47.7 %reduce-scatter.30.cloned.1.call-start = ((), (), s32[]{:S(2)}) async-start(), calls=%async_computation.16 | async-start | bytes 1179648 | tf_op jit(solution)/shard_map/reduce_scatter | solution.py:267
  516.1 5.6 copy-start.50
  516.1 5.6 copy-start.51
  516.1 5.6 copy-start.52
  530.5 41.5 %reduce-scatter.24.cloned.1.call-start = ((), (), s32[]{:S(2)}) async-start(), calls=%async_computation.13 | async-start | bytes 1179648 | tf_op jit(solution)/shard_map/reduce_scatter | solution.py:266
  535.5 4.9 copy-start.30
  542.8 48.8 %reduce-scatter.28.cloned.1.call-start = ((), (), s32[]{:S(2)}) async-start(), calls=%async_computation.15 | async-start | bytes 1179648 | tf_op jit(solution)/shard_map/reduce_scatter | solution.py:266
  550.0 4.8 copy-start.29
  550.0 5.8 copy-start.31
  557.9 160.4 %all-reduce.12.cloned.1.call-start = ((), (), s32[]{:S(2)}) async-start(), calls=%async_computation.24 | async-start | bytes 6291456 | tf_op jit(solution)/shard_map/psum | solution.py:277
  562.0 11.7 %copy-start.55 = (bf16[1,512,192]{1,2,0:T(8,128)(2,1)S(1)}, bf16[1,512,192]{1,2,0:T(8,128)(2,1)}, u32[]{:S(2)}) copy-start(bf16[1,512,192]{1,2,0:T(8,128)(2,1)} %maximum_bitcast_fusion) | copy-start | bytes 589828
  596.7 149.9 %reduce-scatter.44.cloned.1.call-start = ((), (), s32[]{:S(2)}) async-start(), calls=%async_computation.23 | async-start | bytes 442368
  605.3 142.7 %reduce-scatter.38.cloned.1.call-start = ((), (), s32[]{:S(2)}) async-start(), calls=%async_computation.20 | async-start | bytes 884736
  610.3 167.6 %reduce-scatter.36.cloned.1.call-start = ((), (), s32[]{:S(2)}) async-start(), calls=%async_computation.19 | async-start | bytes 2211840
  623.5 162.7 %reduce-scatter.40.cloned.1.call-start = ((), (), s32[]{:S(2)}) async-start(), calls=%async_computation.21 | async-start | bytes 442368
  623.7 4.1 copy-start.123
  623.7 4.7 copy-start.122
  623.7 5.3 copy-start.121
  623.7 5.8 copy-start.120
  718.3 4.2 copy-start.113
  718.3 4.2 copy-start.111
  718.3 4.2 copy-start.24
  718.3 4.2 copy-start.25
  718.3 4.2 copy-start.93
  718.3 4.2 copy-start.106
  718.3 4.2 copy-start.109
  727.1 70.1 %reduce-scatter.42.cloned.1.call-start = ((), (), s32[]{:S(2)}) async-start(), calls=%async_computation.22 | async-start | bytes 442368
  730.2 113.7 %reduce-scatter.34.cloned.1.call-start = ((), (), s32[]{:S(2)}) async-start(), calls=%async_computation.18 | async-start | bytes 2654208 | tf_op jit(solution)/shard_map/reduce_scatter | solution.py:297
  735.1 154.9 %reduce-scatter.32.cloned.1.call-start = ((), (), s32[]{:S(2)}) async-start(), calls=%async_computation.17 | async-start | bytes 2654208 | tf_op jit(solution)/shard_map/reduce_scatter | solution.py:295
  746.5 34.7 %copy-start.94 = (f32[512]{0:T(512)S(1)}, f32[512]{0:T(512)}, u32[]{:S(2)}) copy-start(f32[512]{0:T(512)} %copy-done.92) | copy-start | bytes 6148
  (92 other events, 201.4 us)
Sparse Core Ops, SparseCore 0:
  158.1 121.6 all-reduce.15
  301.6 120.4 all-reduce.13
  424.5 68.4 all-reduce.17
  596.8 121.4 all-reduce.11
Sparse Core Ops, SparseCore 1:
  160.3 24.1 all-gather.7
  186.3 23.8 all-gather.9
  516.1 16.4 reduce-scatter.25
  534.9 17.3 reduce-scatter.29
  554.5 17.4 reduce-scatter.23
  574.3 17.2 reduce-scatter.27
  605.4 34.0 reduce-scatter.43
  642.5 34.9 reduce-scatter.37
  680.7 40.1 reduce-scatter.35
  727.2 32.8 reduce-scatter.39
  763.3 33.8 reduce-scatter.41
  801.5 42.3 reduce-scatter.33
  847.7 42.3 reduce-scatter.31
where the time goes:
time: 906 us; the launch traced here: 898 us
  waiting for transfers between devices  484 us (53%)
  blocking collectives  160 us (18%)
  matrix products  112 us (12%)
  other arithmetic  67.5 us (7%)
  local copies, waits for them, and re-layouts  55.2 us (6%)
  between operations  17.9 us (2%)
    psum x1, waiting for transfers between devices, per_device(): lax.psum(jnp.einsum('cf,df->cd', grad_pre, upward_full, preferred_element...  114 us
    psum x1, waiting for transfers between devices, per_device(): lax.psum(jnp.dot(attended, mixer_weights, preferred_element_type=jnp.floa...  91.5 us
    psum x1, waiting for transfers between devices, per_device(): lax.psum(jnp.einsum('tce,tde->cd', triple, entry_weights, preferred_eleme...  88.1 us
    psum x1, waiting for transfers between devices, per_device(): lax.psum(jnp.dot(activated, downward_full, preferred_element_type=jnp.flo...  66.1 us
    reduce_scatter x1, waiting for transfers between devices, per_device(): lax.psum_scatter(upward_acc, ('dp', 'seq'), scatter_dimension=0, tiled=True)  46.1 us
    unnamed x298, local copies, waits for them, and re-layouts  46 us
    reduce_scatter x1, waiting for transfers between devices, per_device(): lax.psum_scatter(downward_acc, ('dp', 'seq'), scatter_dimension=1, tiled=...  45.3 us
    unnamed x1, blocking collectives  24.1 us
  transfers between devices with their start and end apart: 17, of which 9 were waited for; matrix products, arithmetic and copies ran while one was open for 17% of the time, Pallas kernels for 0%

commit v1 on v0

--- a/solution.py
+++ b/solution.py
@@ -2,6 +2,19 @@
 import jax.numpy as jnp
 from jax import lax
 from jax.sharding import PartitionSpec as P
+
+
+def collect(array, axis, dim):
+    size, place, rows = (lax.axis_size(axis), lax.axis_index(axis), array.shape[dim])
+    right = [(i, (i + 1) % size) for i in range(size)]
+    out = jnp.zeros((*array.shape[:dim], size * rows, *array.shape[dim + 1 :]), array.dtype)
+    held = array
+    for step in range(size):
+        owner = (place - step) % size
+        out = lax.dynamic_update_slice_in_dim(out, held, owner * rows, axis=dim)
+        if step < size - 1:
+            held = lax.ppermute(held, axis, right)
+    return out
 
 
 def norm_rows(values, gain_row, shift_row):
@@ -55,7 +68,7 @@
     results = []
     for batch_index in range(micro):
         gathered = (
-            lax.all_gather(projections, ("dp", "seq"), axis=1, tiled=True),
+            collect(projections, ("dp", "seq"), 1),
             lax.all_gather(offsets, ("dp", "seq"), axis=2, tiled=True),
             lax.all_gather(mixing, ("dp", "seq"), axis=1, tiled=True),
             lax.all_gather(upward, ("dp", "seq"), axis=0, tiled=True),

time: 906 us -> 893 us (0.986)
  starting transfers between devices: 1.52 us -> 13.3 us
    psum x1, waiting for transfers between devices: 114 us -> 91.5 us  [per_device(): lax.psum(jnp.einsum('cf,df->cd', grad_pre, upward_full, preferred_element...]
    ppermute x0 -> x7, waiting for transfers between devices: none -> 15.6 us  [collect(): held = lax.ppermute(held, axis, right)]
    ppermute x0 -> x7, starting transfers between devices: none -> 12.1 us  [collect(): held = lax.ppermute(held, axis, right)]
  transfers between devices with their start and end apart: 17 -> 24, of which waited for: 9 -> 13; matrix products, arithmetic and copies ran while one was open for 17% -> 18% of each run, Pallas kernels for 0% -> 0%
where the time goes in v1:
time: 893 us; the launch traced here: 887 us
  waiting for transfers between devices  476 us (53%)
  blocking collectives  154 us (17%)
  matrix products  103 us (12%)
  other arithmetic  63.9 us (7%)
  local copies, waits for them, and re-layouts  59.1 us (7%)
  between operations  18.3 us (2%)
  starting transfers between devices  13.3 us (1%)
    psum x1, waiting for transfers between devices, per_device(): lax.psum(jnp.einsum('cf,df->cd', grad_pre, upward_full, preferred_element...  91.5 us
    psum x1, waiting for transfers between devices, per_device(): lax.psum(jnp.dot(attended, mixer_weights, preferred_element_type=jnp.floa...  90.7 us
    psum x1, waiting for transfers between devices, per_device(): lax.psum(jnp.einsum('tce,tde->cd', triple, entry_weights, preferred_eleme...  88 us
    psum x1, waiting for transfers between devices, per_device(): lax.psum(jnp.dot(activated, downward_full, preferred_element_type=jnp.flo...  66.1 us
    reduce_scatter x1, waiting for transfers between devices, per_device(): lax.psum_scatter(upward_acc, ('dp', 'seq'), scatter_dimension=0, tiled=True)  46.1 us
    reduce_scatter x1, waiting for transfers between devices, per_device(): lax.psum_scatter(downward_acc, ('dp', 'seq'), scatter_dimension=1, tiled=...  45.2 us
    unnamed x298, local copies, waits for them, and re-layouts  40 us
    unnamed x1, blocking collectives  24.1 us
  transfers between devices with their start and end apart: 24, of which 13 were waited for; matrix products, arithmetic and copies ran while one was open for 18% of the time, Pallas kernels for 0%

profile of v1, /device:TPU:0, one launch (start us, length us, event | category | flops | bytes accessed | tf_op | source)
XLA Modules:
  0.0 887.5 jit_solution(17064295953588478702)
XLA Ops:
  8.1 3.0 collective-permute-start
  11.9 11.4 %all-gather.2 = bf16[8,96,2]{1,2,0:T(2,128)(2,1)S(1)} all-gather(bf16[1,96,2]{1,2,0:T(2,128)(2,1)} %bitcast.295), channel_id=1, replica_groups=mesh['dp'=4,'seq'=2,'tensor'=4] {'dp','seq'}, dimensions={0}, use_global_device_ids=true | all-gather | bytes 3456 | tf_op jit(solution)/shard_map/all_gather | solution.py:77
  23.3 10.9 %all-gather.3 = bf16[8,96,2]{1,2,0:T(2,128)(2,1)S(1)} all-gather(bf16[1,96,2]{1,2,0:T(2,128)(2,1)} %bitcast.296), channel_id=1, replica_groups=mesh['dp'=4,'seq'=2,'tensor'=4] {'dp','seq'}, dimensions={0}, use_global_device_ids=true | all-gather | bytes 3456 | tf_op jit(solution)/shard_map/all_gather | solution.py:78
  35.9 12.5 %all_gather.28 = bf16[2,3,64]{1,0,2:T(2,128)(2,1)S(1)} all-gather(bf16[2,3,8]{1,0,2:T(2,128)(2,1)S(1)} %copy.95), channel_id=1, replica_groups=mesh['dp'=4,'seq'=2,'tensor'=4] {'dp','seq'}, dimensions={2}, use_global_device_ids=true | all-gather | bytes 864 | tf_op jit(solution)/shard_map/all_gather | solution.py:72
  51.6 17.5 %all_gather.31 = bf16[192,768]{0,1:T(8,128)(2,1)S(1)} all-gather(bf16[192,96]{0,1:T(8,128)(2,1)S(1)} %copy.98), channel_id=1, replica_groups=mesh['dp'=4,'seq'=2,'tensor'=4] {'dp','seq'}, dimensions={1}, use_global_device_ids=true | all-gather | bytes 331776 | tf_op jit(solution)/shard_map/all_gather | solution.py:73
  69.9 4.9 collective-permute-done.2
  77.1 3.3 collective-permute-done.3
  82.3 3.6 collective-permute-done.4
  87.7 3.9 collective-permute-done.5
  106.7 6.4 all-gather
  115.5 6.6 all-gather.1
  124.4 7.6 all_gather.71
  132.0 6.3 all_gather.30
  149.3 11.4 %all-gather.4 = bf16[8,96,2]{1,2,0:T(2,128)(2,1)S(1)} all-gather(bf16[1,96,2]{1,2,0:T(2,128)(2,1)S(1)} %bitcast.297), channel_id=1, replica_groups=mesh['dp'=4,'seq'=2,'tensor'=4] {'dp','seq'}, dimensions={0}, use_global_device_ids=true | all-gather | bytes 3456 | tf_op jit(solution)/shard_map/all_gather | solution.py:79
  161.4 16.5 %all_gather.68 = bf16[12,64]{0,1:T(8,128)(2,1)S(1)} all-gather(bf16[12,8]{0,1:T(8,128)(2,1)S(1)} %copy-done.131), channel_id=1, replica_groups=mesh['dp'=4,'seq'=2,'tensor'=4] {'dp','seq'}, dimensions={1}, use_global_device_ids=true | all-gather | bytes 1728 | tf_op jit(solution)/shard_map/all_gather | solution.py:75
  178.6 90.7 %all-reduce.16.cloned.1.call-done = (f32[512,768]{1,0:T(8,128)}, f32[512,768]{1,0:T(8,128)}) async-done(((f32[512,768]{1,0:T(8,128)}, f32[512,768]{1,0:T(8,128)}), (f32[512,768]{1,0:T(8,128)}, f32[512,768]{1,0:T(8,128)})) %all-reduce.16.cloned.1.call-update) | async-done | bytes 3145744 | tf_op jit(solution)/shard_map/psum | solution.py:124
  269.4 2.4 fusion.182
  274.1 3.9 convolution_add_fusion.3
  278.0 2.1 convolution_add_fusion.2
  280.2 4.5 convert_reduce_fusion.5
  284.7 2.4 convert_reduce_fusion.4
  287.1 2.0 fusion.195
  291.2 3.9 convolution_convert_fusion.1
  297.1 23.1 %all_gather.72 = bf16[3,768,192]{2,1,0:T(8,128)(2,1)} all-gather(bf16[3,96,192]{2,1,0:T(8,128)(2,1)} %param.14), channel_id=1, replica_groups=mesh['dp'=4,'seq'=2,'tensor'=4] {'dp','seq'}, dimensions={1}, use_global_device_ids=true | all-gather | bytes 995328 | tf_op jit(solution)/shard_map/all_gather | solution.py:168
  320.2 91.5 %all-reduce.14.cloned.1.call-done = (f32[512,768]{1,0:T(8,128)}, f32[512,768]{1,0:T(8,128)}) async-done(((f32[512,768]{1,0:T(8,128)}, f32[512,768]{1,0:T(8,128)}), (f32[512,768]{1,0:T(8,128)}, f32[512,768]{1,0:T(8,128)})) %all-reduce.14.cloned.1.call-update) | async-done | bytes 3145744 | tf_op jit(solution)/shard_map/psum | solution.py:220
  411.8 3.6 multiply_reduce_fusion.6
  416.6 66.1 %all-reduce.18.cloned.1.call-done = (bf16[512,768]{1,0:T(8,128)(2,1)}, bf16[512,768]{1,0:T(8,128)(2,1)}) async-done(((bf16[512,768]{1,0:T(8,128)(2,1)}, bf16[512,768]{1,0:T(8,128)(2,1)}), (bf16[512,768]{1,0:T(8,128)(2,1)}, bf16[512,768]{1,0:T(8,128)(2,1)})) %all-reduce.18.cloned.1.call-update) | async-done | bytes 1572880 | tf_op jit(solution)/shard_map/psum | solution.py:133
  482.7 5.0 fusion.181
  499.9 2.4 multiply_reduce_fusion.3
  502.4 2.4 multiply_reduce_fusion.4
  505.8 2.8 multiply_convert_fusion.3
  512.4 2.8 multiply_convert_fusion.4
  520.3 2.1 pad_maximum_fusion.2
  522.4 2.3 multiply_reduce_fusion
  525.3 2.4 convolution_multiply_fusion
  527.7 2.4 multiply_reduce_fusion.1
  530.1 2.4 multiply_reduce_fusion.2
  532.8 2.8 multiply_convert_fusion.1
  539.5 2.5 fusion.50
  542.0 2.3 fusion.49
  554.9 6.7 reduce-scatter.24.cloned.1.call-done
  563.3 3.4 convolution_bitcast_fusion.1
  566.7 14.6 %reduce-scatter.28.cloned.1.call-done = f32[512,192]{0,1:T(8,128)} async-done(((f32[1024,192]{0,1:T(8,128)}), f32[512,192]{0,1:T(8,128)}) %reduce-scatter.28.cloned.1.call-update) | async-done | bytes 393232 | tf_op jit(solution)/shard_map/reduce_scatter | solution.py:279
  583.0 3.4 convolution_bitcast_fusion
  587.1 2.5 fusion.179
  591.9 3.2 fusion.85
  595.1 2.7 convolution_add_fusion.4
  597.8 2.2 copy.108
  602.2 2.1 add_bitcast_fusion
  604.3 4.2 copy.104
  608.5 4.7 reshape.314
  613.6 4.1 fusion.65
  620.0 88.0 %all-reduce.12.cloned.1.call-done = (f32[512,768]{1,0:T(8,128)}, f32[512,768]{1,0:T(8,128)}) async-done(((f32[512,768]{1,0:T(8,128)}, f32[512,768]{1,0:T(8,128)}), (f32[512,768]{1,0:T(8,128)}, f32[512,768]{1,0:T(8,128)})) %all-reduce.12.cloned.1.call-update) | async-done | bytes 3145744 | tf_op jit(solution)/shard_map/psum | solution.py:290
  708.1 2.9 fusion.31
  712.3 2.3 fusion.29
  720.0 4.9 convolution_add_fusion
  725.0 2.8 fusion.177
  727.9 2.5 convolution_add_fusion.1
  733.6 2.7 pad_maximum_fusion
  742.1 24.1 %all-reduce.2 = (f32[2,3,64]{2,1,0:T(4,128)S(1)}, f32[12,64]{1,0:T(8,128)S(1)}) all-reduce(f32[2,3,64]{2,1,0:T(4,128)S(1)} %maximum_add_fusion.3, f32[12,64]{1,0:T(8,128)} %add.493), channel_id=9, replica_groups=mesh['dp'=4,'seq'=2,'tensor'=4] {'dp','seq'}, use_global_device_ids=true, to_apply=%region_49.50.clone | all-reduce | flops 1152 | bytes 9216
  770.9 3.7 fusion.56
  777.3 9.7 %reduce-scatter.42.cloned.1.call-done = f32[96,2]{1,0:T(8,128)} async-done(((f32[768,2]{1,0:T(8,128)}), f32[96,2]{1,0:T(8,128)}) %reduce-scatter.42.cloned.1.call-update) | async-done | bytes 784
  788.5 45.2 %reduce-scatter.34.cloned.1.call-done = f32[768,96]{0,1:T(8,128)} async-done(((f32[768,768]{0,1:T(8,128)}), f32[768,96]{0,1:T(8,128)}) %reduce-scatter.34.cloned.1.call-update) | async-done | bytes 294928 | tf_op jit(solution)/shard_map/reduce_scatter | solution.py:310
  833.7 46.1 %reduce-scatter.32.cloned.1.call-done = f32[96,768]{1,0:T(8,128)} async-done(((f32[768,768]{1,0:T(8,128)}), f32[96,768]{1,0:T(8,128)}) %reduce-scatter.32.cloned.1.call-update) | async-done | bytes 294928 | tf_op jit(solution)/shard_map/reduce_scatter | solution.py:308
  (498 shorter events, 124.0 us)
Async XLA Ops:
  8.0 40.5 %copy-start = (bf16[2,512,768]{2,1,0:T(8,128)(2,1)S(1)}, bf16[2,512,768]{2,1,0:T(8,128)(2,1)}, u32[]{:S(2)}) copy-start(bf16[2,512,768]{2,1,0:T(8,128)(2,1)} %param.12) | copy-start | bytes 4718596
  8.0 27.9 %copy-start.127 = (s32[2,1024]{1,0:T(2,128)S(1)}, s32[2,1024]{1,0:T(2,128)}, u32[]{:S(2)}) copy-start(s32[2,1024]{1,0:T(2,128)} %param.13) | copy-start | bytes 24580
  8.0 261.3 %all-reduce.16.cloned.1.call-start = ((), (), s32[]{:S(2)}) async-start(), calls=%async_computation.26 | async-start | bytes 6291456 | tf_op jit(solution)/shard_map/psum | solution.py:124
  8.1 41.1 %collective-permute-start = (bf16[3,96,192]{2,1,0:T(8,128)(2,1)}, bf16[3,96,192]{2,1,0:T(8,128)(2,1)S(1)}, u32[]{:S(2)}, u32[]{:S(2)}) collective-permute-start(bf16[3,96,192]{2,1,0:T(8,128)(2,1)} %param.14), channel_id=1, source_target_pairs={{0,4},{4,8},{8,12},{12,16},{16,20},{20,24},{24,28},{28,0},{1,5},{5... | collective-permute-start | bytes 331784 | tf_op jit(solution)/shard_map/ppermute | solution.py:16
  34.2 15.9 %copy-start.67 = (bf16[3,96,192]{2,1,0:T(8,128)(2,1)S(1)}, bf16[3,96,192]{2,1,0:T(8,128)(2,1)}, u32[]{:S(2)}) copy-start(bf16[3,96,192]{2,1,0:T(8,128)(2,1)} %param.14) | copy-start | bytes 331780
  35.9 14.9 %copy-start.99 = (bf16[192,96]{1,0:T(8,128)(2,1)S(1)}, bf16[192,96]{1,0:T(8,128)(2,1)}, u32[]{:S(2)}) copy-start(bf16[192,96]{1,0:T(8,128)(2,1)} %param.16) | copy-start | bytes 110596
  48.5 56.4 %copy-start.90 = (f32[512]{0:T(512)}, f32[512]{0:T(512)S(1)}, u32[]{:S(2)}) copy-start(f32[512]{0:T(512)S(1)} %get-tuple-element.168) | copy-start | bytes 6148
  48.5 57.3 %copy-start.92 = (f32[512]{0:T(512)}, f32[512]{0:T(512)S(1)}, u32[]{:S(2)}) copy-start(f32[512]{0:T(512)S(1)} %get-tuple-element.169) | copy-start | bytes 6148
  49.1 56.6 %copy-start.105 = (f32[512]{0:T(512)}, f32[512]{0:T(512)S(1)}, u32[]{:S(2)}) copy-start(f32[512]{0:T(512)S(1)} %fusion.150) | copy-start | bytes 6148
  49.2 20.0 %collective-permute-start.1 = (bf16[3,96,192]{2,1,0:T(8,128)(2,1)S(1)}, bf16[3,96,192]{2,1,0:T(8,128)(2,1)S(1)}, u32[]{:S(2)}, u32[]{:S(2)}) collective-permute-start(bf16[3,96,192]{2,1,0:T(8,128)(2,1)S(1)} %collective-permute-done), channel_id=1, source_target_pairs={{0,4},{4,8},{8,12},{12,16},{16,20},{20,24},{24,28},{28,0},{1,5},{5... | collective-permute-start | bytes 331784 | tf_op jit(solution)/shard_map/ppermute | solution.py:16
  50.1 54.7 %copy-start.107 = (f32[512]{0:T(512)}, f32[512]{0:T(512)S(1)}, u32[]{:S(2)}) copy-start(f32[512]{0:T(512)S(1)} %fusion.152) | copy-start | bytes 6148
  69.1 5.6 collective-permute-start.2
  74.7 5.6 collective-permute-start.3
  77.1 28.7 %copy-start.128 = (f32[768]{0:T(1024)}, f32[768]{0:T(1024)S(1)}, u32[]{:S(2)}) copy-start(f32[768]{0:T(1024)S(1)} %get-tuple-element.95) | copy-start | bytes 9220
  80.3 13.2 %copy-start.72 = (bf16[3,96,192]{2,1,0:T(8,128)(2,1)}, bf16[3,96,192]{2,1,0:T(8,128)(2,1)S(1)}, u32[]{:S(2)}) copy-start(bf16[3,96,192]{2,1,0:T(8,128)(2,1)S(1)} %collective-permute-done.3) | copy-start | bytes 331780
  80.3 5.6 collective-permute-start.4
  85.9 7.6 copy-start.74
  85.9 5.7 collective-permute-start.5
  91.6 10.9 %collective-permute-start.6 = (bf16[3,96,192]{2,1,0:T(8,128)(2,1)}, bf16[3,96,192]{2,1,0:T(8,128)(2,1)}, u32[]{:S(2)}, u32[]{:S(2)}) collective-permute-start(bf16[3,96,192]{2,1,0:T(8,128)(2,1)} %collective-permute-done.5), channel_id=1, source_target_pairs={{0,4},{4,8},{8,12},{12,16},{16,20},{20,24},{24,28},{28,0},{1,5},{5... | collective-permute-start | bytes 331784 | tf_op jit(solution)/shard_map/ppermute | solution.py:16
  113.2 10.5 %copy-start.60 = (bf16[512,192]{0,1:T(8,128)(2,1)}, bf16[512,192]{0,1:T(8,128)(2,1)S(1)}, u32[]{:S(2)}) copy-start(bf16[512,192]{0,1:T(8,128)(2,1)S(1)} %get-tuple-element.126) | copy-start | bytes 589828
  114.0 25.4 %copy-start.16 = (f32[512,1024]{1,0:T(8,128)}, f32[512,1024]{1,0:T(8,128)S(1)}, u32[]{:S(2)}) copy-start(f32[512,1024]{1,0:T(8,128)S(1)} %get-tuple-element.147) | copy-start | bytes 6291460
  114.8 25.2 %copy-start.14 = (f32[512,1024]{1,0:T(8,128)}, f32[512,1024]{1,0:T(8,128)S(1)}, u32[]{:S(2)}) copy-start(f32[512,1024]{1,0:T(8,128)S(1)} %get-tuple-element.149) | copy-start | bytes 6291460
  115.5 25.5 %copy-start.11 = (f32[512,1024]{1,0:T(8,128)}, f32[512,1024]{1,0:T(8,128)S(1)}, u32[]{:S(2)}) copy-start(f32[512,1024]{1,0:T(8,128)S(1)} %get-tuple-element.151) | copy-start | bytes 6291460
  122.9 19.8 %copy-start.8 = (f32[512,1024]{1,0:T(8,128)}, f32[512,1024]{1,0:T(8,128)S(1)}, u32[]{:S(2)}) copy-start(f32[512,1024]{1,0:T(8,128)S(1)} %get-tuple-element.141) | copy-start | bytes 6291460
  123.7 19.6 %copy-start.5 = (f32[512,1024]{1,0:T(8,128)}, f32[512,1024]{1,0:T(8,128)S(1)}, u32[]{:S(2)}) copy-start(f32[512,1024]{1,0:T(8,128)S(1)} %get-tuple-element.143) | copy-start | bytes 6291460
  124.4 19.9 %copy-start.1 = (f32[512,1024]{1,0:T(8,128)}, f32[512,1024]{1,0:T(8,128)S(1)}, u32[]{:S(2)}) copy-start(f32[512,1024]{1,0:T(8,128)S(1)} %get-tuple-element.145) | copy-start | bytes 6291460
  132.0 12.3 %copy-start.38 = (bf16[1024,192]{0,1:T(8,128)(2,1)}, bf16[1024,192]{0,1:T(8,128)(2,1)S(1)}, u32[]{:S(2)}) copy-start(bf16[1024,192]{0,1:T(8,128)(2,1)S(1)} %all_gather.71) | copy-start | bytes 1179652
  140.0 4.9 copy-start.68
  148.1 13.3 %copy-start.131 = (bf16[12,8]{0,1:T(8,128)(2,1)S(1)}, bf16[12,8]{0,1:T(8,128)(2,1)}, u32[]{:S(2)}) copy-start(bf16[12,8]{0,1:T(8,128)(2,1)} %param.18) | copy-start | bytes 580
  148.1 126.0 %all-gather.8.cloned.1.call-start = ((), (), s32[]{:S(2)}) async-start(), calls=%async_computation.11 | async-start | bytes 1327104 | tf_op jit(solution)/shard_map/all_gather | solution.py:74
  148.7 131.5 %all-gather.10.cloned.1.call-start = ((), (), s32[]{:S(2)}) async-start(), calls=%async_computation.12 | async-start | bytes 1327104 | tf_op jit(solution)/shard_map/all_gather | solution.py:76
  149.3 262.5 %all-reduce.14.cloned.1.call-start = ((), (), s32[]{:S(2)}) async-start(), calls=%async_computation.25 | async-start | bytes 6291456 | tf_op jit(solution)/shard_map/psum | solution.py:220
  271.7 140.0 %copy-start.19 = (f32[512,768]{1,0:T(8,128)}, f32[512,768]{1,0:T(8,128)S(1)}, u32[]{:S(2)}) copy-start(f32[512,768]{1,0:T(8,128)S(1)} %get-tuple-element.121) | copy-start | bytes 4718596
  271.8 210.9 %copy-start.97 = (f32[512]{0:T(512)}, f32[512]{0:T(512)S(1)}, u32[]{:S(2)}) copy-start(f32[512]{0:T(512)S(1)} %broadcast_multiply_fusion) | copy-start | bytes 6148
  280.2 4.5 copy-start.21
  280.2 4.5 copy-start.36
  280.2 4.5 copy-start.133
  284.7 4.5 copy-start.138
  291.2 191.6 %all-reduce.18.cloned.1.call-start = ((), (), s32[]{:S(2)}) async-start(), calls=%async_computation.27 | async-start | bytes 3145728 | tf_op jit(solution)/shard_map/psum | solution.py:133
  297.1 254.4 %reduce-scatter.26.cloned.1.call-start = ((), (), s32[]{:S(2)}) async-start(), calls=%async_computation.14 | async-start | bytes 1179648 | tf_op jit(solution)/shard_map/reduce_scatter | solution.py:280
  482.7 5.6 copy-start.22
  489.8 12.5 %copy-start.44 = (bf16[512,192]{0,1:T(8,128)(2,1)}, bf16[512,192]{0,1:T(8,128)(2,1)S(1)}, u32[]{:S(2)}) copy-start(bf16[512,192]{0,1:T(8,128)(2,1)S(1)} %convolution_convert_fusion.3) | copy-start | bytes 589828
  505.7 47.5 %reduce-scatter.30.cloned.1.call-start = ((), (), s32[]{:S(2)}) async-start(), calls=%async_computation.16 | async-start | bytes 1179648 | tf_op jit(solution)/shard_map/reduce_scatter | solution.py:280
  505.7 5.7 copy-start.50
  505.8 5.7 copy-start.51
  505.8 5.7 copy-start.52
  520.3 41.3 %reduce-scatter.24.cloned.1.call-start = ((), (), s32[]{:S(2)}) async-start(), calls=%async_computation.13 | async-start | bytes 1179648 | tf_op jit(solution)/shard_map/reduce_scatter | solution.py:279
  525.3 4.9 copy-start.30
  532.5 48.8 %reduce-scatter.28.cloned.1.call-start = ((), (), s32[]{:S(2)}) async-start(), calls=%async_computation.15 | async-start | bytes 1179648 | tf_op jit(solution)/shard_map/reduce_scatter | solution.py:279
  539.5 4.8 copy-start.29
  539.5 5.9 copy-start.31
  547.4 160.6 %all-reduce.12.cloned.1.call-start = ((), (), s32[]{:S(2)}) async-start(), calls=%async_computation.24 | async-start | bytes 6291456 | tf_op jit(solution)/shard_map/psum | solution.py:290
  551.4 11.9 %copy-start.53 = (bf16[1,512,192]{1,2,0:T(8,128)(2,1)S(1)}, bf16[1,512,192]{1,2,0:T(8,128)(2,1)}, u32[]{:S(2)}) copy-start(bf16[1,512,192]{1,2,0:T(8,128)(2,1)} %maximum_bitcast_fusion) | copy-start | bytes 589828
  586.4 149.8 %reduce-scatter.44.cloned.1.call-start = ((), (), s32[]{:S(2)}) async-start(), calls=%async_computation.23 | async-start | bytes 442368
  595.1 142.6 %reduce-scatter.38.cloned.1.call-start = ((), (), s32[]{:S(2)}) async-start(), calls=%async_computation.20 | async-start | bytes 884736
  600.1 167.5 %reduce-scatter.36.cloned.1.call-start = ((), (), s32[]{:S(2)}) async-start(), calls=%async_computation.19 | async-start | bytes 2211840
  613.3 162.6 %reduce-scatter.40.cloned.1.call-start = ((), (), s32[]{:S(2)}) async-start(), calls=%async_computation.21 | async-start | bytes 442368
  613.6 4.7 copy-start.122
  613.6 5.3 copy-start.121
  613.6 5.9 copy-start.120
  716.9 70.1 %reduce-scatter.42.cloned.1.call-start = ((), (), s32[]{:S(2)}) async-start(), calls=%async_computation.22 | async-start | bytes 442368
  719.9 113.7 %reduce-scatter.34.cloned.1.call-start = ((), (), s32[]{:S(2)}) async-start(), calls=%async_computation.18 | async-start | bytes 2654208 | tf_op jit(solution)/shard_map/reduce_scatter | solution.py:310
  724.9 154.9 %reduce-scatter.32.cloned.1.call-start = ((), (), s32[]{:S(2)}) async-start(), calls=%async_computation.17 | async-start | bytes 2654208 | tf_op jit(solution)/shard_map/reduce_scatter | solution.py:308
  736.2 34.7 %copy-start.94 = (f32[512]{0:T(512)S(1)}, f32[512]{0:T(512)}, u32[]{:S(2)}) copy-start(f32[512]{0:T(512)} %copy-done.92) | copy-start | bytes 6148
  (99 other events, 240.0 us)
Sparse Core Ops, SparseCore 0:
  148.2 121.0 all-reduce.15
  291.3 120.4 all-reduce.13
  414.2 68.4 all-reduce.17
  586.5 121.4 all-reduce.11
Sparse Core Ops, SparseCore 1:
  150.5 23.5 all-gather.7
  175.8 23.9 all-gather.9
  505.8 16.4 reduce-scatter.25
  524.6 17.3 reduce-scatter.29
  544.2 17.3 reduce-scatter.23
  563.9 17.3 reduce-scatter.27
  595.1 34.0 reduce-scatter.43
  632.3 35.0 reduce-scatter.37
  670.6 40.1 reduce-scatter.35
  717.0 32.8 reduce-scatter.39
  753.1 33.8 reduce-scatter.41
  791.3 42.3 reduce-scatter.33
  837.5 42.3 reduce-scatter.31
